TPU v7x, 32 devices: a whole 2x2x4 slice. The times are simulated.
32 devices in a mesh: row: 4 (over x, core), col: 8 (over z, y).
Axes of the slice: x: 2, y: 2, z: 4, core: 2. Of those that a mesh axis runs over, the one named last changes fastest.
Arguments:
- vectors: float32 [8, 4096], P(None, ('row', 'col')), may hold values from -6 to 6
- diagonal: float32 [4096], P(('row', 'col'))
- blocks: float32 [4, 8, 8, 128, 128], P('row', 'col'), may hold values from -0.125 to 0.125
- block_rows: int32 [4, 8, 8], P('row', 'col'), may hold values from 0 to 7
- block_cols: int32 [4, 8, 8], P('row', 'col'), may hold values from 0 to 3
- counts: int32 [4, 8], P('row', 'col'), may hold values from 4 to 8, as said below
Outputs:
- eigvecs: float32 [8, 4096], P(None, ('row', 'col'))
- factor: float32 [8, 8], replicated
Inputs may be any that keep to these rules, and one draw needn't show every extreme that they name: `counts`: every device has at least half of its 8 slots live, and some device has all 8 live.
All inputs are finite; a program needn't handle non-finite values.
Results may differ from a plain program's by a relative error of at most 0.0001.
Values sent between devices are 32-bit elements; how exact they have to be, the bound alone decides.
No kernel may reach another device: no remote copies, remote signals or barrier semaphores. Data moves between devices by JAX's collectives and lax.ppermute only.
A program may use at most 64 MiB of HBM per device.

v0:
```python
import jax
import jax.numpy as jnp
from jax import lax
from jax.sharding import PartitionSpec as P

ITERS = 4


def solve_lower(lower, values):
    return lax.linalg.triangular_solve(lower, values, left_side=True, lower=True)


def apply_tile(tile, rows_local, cols_local, live, current, col_vectors, row_vectors):
    high = lax.Precision.HIGHEST
    nvec = current.shape[0]
    width = tile.shape[-1]
    col_count = col_vectors.shape[1] // width
    row_count = row_vectors.shape[1] // width
    slots = jnp.arange(rows_local.shape[0])
    mask = (slots < live).astype(jnp.float32)
    row_select = (rows_local[:, None] == jnp.arange(row_count)[None, :]).astype(jnp.float32) * mask[
        :, None
    ]
    col_select = (cols_local[:, None] == jnp.arange(col_count)[None, :]).astype(jnp.float32) * mask[
        :, None
    ]
    col_input = jnp.einsum(
        "bq,kqj->kbj", col_select, col_vectors.reshape(nvec, col_count, width), precision=high
    )
    direct = jnp.einsum("bij,kbj->kbi", tile, col_input, precision=high)
    direct_part = jnp.einsum("bq,kbi->kqi", row_select, direct, precision=high).reshape(
        nvec, row_count * width
    )
    row_input = jnp.einsum(
        "bq,kqi->kbi", row_select, row_vectors.reshape(nvec, row_count, width), precision=high
    )
    transposed = jnp.einsum("bij,kbi->kbj", tile, row_input, precision=high)
    transposed_part = jnp.einsum("bq,kbj->kqj", col_select, transposed, precision=high).reshape(
        nvec, col_count * width
    )
    direct_sum = lax.psum_scatter(direct_part, "col", scatter_dimension=1, tiled=True)
    transposed_sum = lax.psum_scatter(transposed_part, "row", scatter_dimension=1, tiled=True)
    return (direct_sum, transposed_sum)


def gram_factor(images):
    local_gram = jnp.dot(
        images, images.T, precision=lax.Precision.HIGHEST, preferred_element_type=jnp.float32
    )
    gram = lax.psum(local_gram, ("row", "col"))
    return jnp.linalg.cholesky(gram)


def shards(vectors, diagonal, blocks, block_rows, block_cols, counts):
    tile = blocks[0, 0]
    rows_local = block_rows[0, 0]
    cols_local = block_cols[0, 0]
    live = counts[0, 0]
    nvec = vectors.shape[0]
    current = vectors
    lower = jnp.eye(nvec, dtype=jnp.float32)
    for step in range(ITERS):
        col_vectors = lax.all_gather(current, "row", axis=1, tiled=True)
        row_vectors = lax.all_gather(current, "col", axis=1, tiled=True)
        direct_sum, transposed_sum = apply_tile(
            tile, rows_local, cols_local, live, current, col_vectors, row_vectors
        )
        images = diagonal[None, :] * current + direct_sum + transposed_sum
        lower = gram_factor(images)
        current = solve_lower(lower, images)
    return (current, lower)


def solution(mesh):
    placed = (
        P(None, ("row", "col")),
        P(("row", "col")),
        P("row", "col", None, None, None),
        P("row", "col", None),
        P("row", "col", None),
        P("row", "col"),
    )
    return jax.shard_map(
        shards,
        mesh=mesh,
        in_specs=placed,
        out_specs=(P(None, ("row", "col")), P()),
        check_vma=False,
    )
```

profile of v0, /device:TPU:0, one launch (start us, length us, event | category | flops | bytes accessed | tf_op | source)
XLA Modules:
  0.0 656.2 jit_solution(13595704017735790086)
XLA Ops:
  7.9 32.4 %all_gather.25 = f32[8,1024]{1,0:T(8,128)S(1)} all-gather(f32[8,128]{1,0:T(8,128)S(1)} %copy-done.1), channel_id=1, replica_groups=mesh['row'=4,'col'=8] {'col'}, dimensions={1}, use_global_device_ids=true | all-gather | bytes 36864 | tf_op jit(solution)/shard_map/all_gather | solution.py:64
  40.4 0.7 copy-done.3
  41.8 0.7 copy-done.2
  43.3 5.2 all_gather.24
  48.7 0.9 fusion.14
  50.5 13.4 %reduce-scatter.11.cloned.1.call-done = f32[8,128]{1,0:T(8,128)} async-done(((f32[8,512]{1,0:T(8,128)}), f32[8,128]{1,0:T(8,128)}) %reduce-scatter.11.cloned.1.call-update) | async-done | bytes 4112 | tf_op jit(solution)/shard_map/reduce_scatter | solution.py:42
  63.9 57.9 %reduce-scatter.9.cloned.1.call-done = f32[8,128]{1,0:T(8,128)} async-done(((f32[8,1024]{1,0:T(8,128)}), f32[8,128]{1,0:T(8,128)}) %reduce-scatter.9.cloned.1.call-update) | async-done | bytes 4112 | tf_op jit(solution)/shard_map/reduce_scatter | solution.py:41
  121.8 0.7 add_add_fusion.3
  122.6 40.1 %psum.28 = f32[8,8]{0,1:T(8,128)S(1)} all-reduce(f32[8,8]{0,1:T(8,128)S(1)} %fusion.165), channel_id=1, replica_groups=mesh['row'=4,'col'=8] {'row','col'}, use_global_device_ids=true, to_apply=%region_2.0 | all-reduce | flops 64 | bytes 512 | tf_op jit(solution)/shard_map/psum | solution.py:50
  162.8 0.7 cholesky.74
  163.5 0.6 compare_reduce_fusion.3
  164.2 0.6 fusion.46
  165.7 5.5 all_gather.26
  171.2 30.6 %all_gather.27 = f32[8,1024]{1,0:T(8,128)S(1)} all-gather(f32[8,128]{1,0:T(8,128)S(1)} %fusion.55), channel_id=1, replica_groups=mesh['row'=4,'col'=8] {'col'}, dimensions={1}, use_global_device_ids=true | all-gather | bytes 36864 | tf_op jit(solution)/shard_map/all_gather | solution.py:64
  201.8 1.0 convolution_bitcast_fusion.5
  203.0 0.9 fusion.10
  203.9 1.0 convolution_bitcast_fusion.2
  207.3 17.4 %reduce-scatter.15.cloned.1.call-done = f32[8,128]{1,0:T(8,128)} async-done(((f32[8,512]{1,0:T(8,128)}), f32[8,128]{1,0:T(8,128)}) %reduce-scatter.15.cloned.1.call-update) | async-done | bytes 4112 | tf_op jit(solution)/shard_map/reduce_scatter | solution.py:42
  224.7 57.8 %reduce-scatter.13.cloned.1.call-done = f32[8,128]{1,0:T(8,128)} async-done(((f32[8,1024]{1,0:T(8,128)}), f32[8,128]{1,0:T(8,128)}) %reduce-scatter.13.cloned.1.call-update) | async-done | bytes 4112 | tf_op jit(solution)/shard_map/reduce_scatter | solution.py:41
  282.5 0.7 add_add_fusion.2
  283.3 40.1 %psum.29 = f32[8,8]{0,1:T(8,128)S(1)} all-reduce(f32[8,8]{0,1:T(8,128)S(1)} %fusion.166), channel_id=1, replica_groups=mesh['row'=4,'col'=8] {'row','col'}, use_global_device_ids=true, to_apply=%region_7.10 | all-reduce | flops 64 | bytes 512 | tf_op jit(solution)/shard_map/psum | solution.py:50
  323.5 0.7 cholesky.85
  324.2 0.6 compare_reduce_fusion.2
  324.9 0.6 fusion.47
  326.4 5.5 all_gather.28
  331.9 30.6 %all_gather.29 = f32[8,1024]{1,0:T(8,128)S(1)} all-gather(f32[8,128]{1,0:T(8,128)S(1)} %fusion.53), channel_id=1, replica_groups=mesh['row'=4,'col'=8] {'col'}, dimensions={1}, use_global_device_ids=true | all-gather | bytes 36864 | tf_op jit(solution)/shard_map/all_gather | solution.py:64
  362.5 1.0 convolution_bitcast_fusion.4
  363.7 0.9 fusion.6
  364.6 1.0 convolution_bitcast_fusion.1
  368.0 17.4 %reduce-scatter.19.cloned.1.call-done = f32[8,128]{1,0:T(8,128)} async-done(((f32[8,512]{1,0:T(8,128)}), f32[8,128]{1,0:T(8,128)}) %reduce-scatter.19.cloned.1.call-update) | async-done | bytes 4112 | tf_op jit(solution)/shard_map/reduce_scatter | solution.py:42
  385.4 57.8 %reduce-scatter.17.cloned.1.call-done = f32[8,128]{1,0:T(8,128)} async-done(((f32[8,1024]{1,0:T(8,128)}), f32[8,128]{1,0:T(8,128)}) %reduce-scatter.17.cloned.1.call-update) | async-done | bytes 4112 | tf_op jit(solution)/shard_map/reduce_scatter | solution.py:41
  443.2 0.7 add_add_fusion.1
  444.1 40.3 %psum.30 = f32[8,8]{0,1:T(8,128)S(1)} all-reduce(f32[8,8]{0,1:T(8,128)S(1)} %fusion.167), channel_id=1, replica_groups=mesh['row'=4,'col'=8] {'row','col'}, use_global_device_ids=true, to_apply=%region_10.13 | all-reduce | flops 64 | bytes 512 | tf_op jit(solution)/shard_map/psum | solution.py:50
  484.4 0.7 cholesky.96
  485.1 0.6 compare_reduce_fusion.1
  485.8 0.6 fusion.48
  487.3 5.5 all_gather.30
  492.8 30.6 %all_gather.31 = f32[8,1024]{1,0:T(8,128)S(1)} all-gather(f32[8,128]{1,0:T(8,128)S(1)} %fusion.51), channel_id=1, replica_groups=mesh['row'=4,'col'=8] {'col'}, dimensions={1}, use_global_device_ids=true | all-gather | bytes 36864 | tf_op jit(solution)/shard_map/all_gather | solution.py:64
  523.4 1.0 convolution_bitcast_fusion.3
  524.6 0.9 fusion.2
  525.5 1.0 convolution_bitcast_fusion
  528.9 17.5 %reduce-scatter.23.cloned.1.call-done = f32[8,128]{1,0:T(8,128)} async-done(((f32[8,512]{1,0:T(8,128)}), f32[8,128]{1,0:T(8,128)}) %reduce-scatter.23.cloned.1.call-update) | async-done | bytes 4112 | tf_op jit(solution)/shard_map/reduce_scatter | solution.py:42
  546.4 57.9 %reduce-scatter.21.cloned.1.call-done = f32[8,128]{1,0:T(8,128)} async-done(((f32[8,1024]{1,0:T(8,128)}), f32[8,128]{1,0:T(8,128)}) %reduce-scatter.21.cloned.1.call-update) | async-done | bytes 4112 | tf_op jit(solution)/shard_map/reduce_scatter | solution.py:41
  604.3 0.7 add_add_fusion
  605.1 40.1 %psum.31 = f32[8,8]{0,1:T(8,128)S(1)} all-reduce(f32[8,8]{0,1:T(8,128)S(1)} %fusion.168), channel_id=1, replica_groups=mesh['row'=4,'col'=8] {'row','col'}, use_global_device_ids=true, to_apply=%region_13.16 | all-reduce | flops 64 | bytes 512 | tf_op jit(solution)/shard_map/psum | solution.py:50
  645.3 0.7 cholesky.107
  646.7 1.2 select_bitcast_fusion
  648.6 0.8 fusion.49
  (77 shorter events, 15.0 us)
Async XLA Ops:
  7.2 34.1 %copy-start = (f32[1,1,8,128,128]{4,3,2,1,0:T(8,128)S(1)}, f32[1,1,8,128,128]{4,3,2,1,0:T(8,128)}, u32[]{:S(2)}) copy-start(f32[1,1,8,128,128]{4,3,2,1,0:T(8,128)} %param.11) | copy-start | bytes 1572868
  7.2 0.8 copy-start.1
  7.2 56.7 %reduce-scatter.11.cloned.1.call-start = ((), (), s32[]{:S(2)}) async-start(), calls=%async_computation.9 | async-start | bytes 20480 | tf_op jit(solution)/shard_map/reduce_scatter | solution.py:42
  40.4 0.7 copy-start.3
  41.8 0.7 copy-start.2
  43.2 78.5 %reduce-scatter.9.cloned.1.call-start = ((), (), s32[]{:S(2)}) async-start(), calls=%async_computation.8 | async-start | bytes 36864 | tf_op jit(solution)/shard_map/reduce_scatter | solution.py:41
  50.5 71.3 %copy-start.4 = (f32[128]{0:T(128)S(1)}, f32[128]{0:T(128)}, u32[]{:S(2)}) copy-start(f32[128]{0:T(128)} %param.10) | copy-start | bytes 1540
  50.5 174.3 %reduce-scatter.15.cloned.1.call-start = ((), (), s32[]{:S(2)}) async-start(), calls=%async_computation.11 | async-start | bytes 20480 | tf_op jit(solution)/shard_map/reduce_scatter | solution.py:42
  206.4 76.0 %reduce-scatter.13.cloned.1.call-start = ((), (), s32[]{:S(2)}) async-start(), calls=%async_computation.10 | async-start | bytes 36864 | tf_op jit(solution)/shard_map/reduce_scatter | solution.py:41
  207.3 178.1 %reduce-scatter.19.cloned.1.call-start = ((), (), s32[]{:S(2)}) async-start(), calls=%async_computation.13 | async-start | bytes 20480 | tf_op jit(solution)/shard_map/reduce_scatter | solution.py:42
  367.1 76.1 %reduce-scatter.17.cloned.1.call-start = ((), (), s32[]{:S(2)}) async-start(), calls=%async_computation.12 | async-start | bytes 36864 | tf_op jit(solution)/shard_map/reduce_scatter | solution.py:41
  368.0 178.4 %reduce-scatter.23.cloned.1.call-start = ((), (), s32[]{:S(2)}) async-start(), calls=%async_computation.15 | async-start | bytes 20480 | tf_op jit(solution)/shard_map/reduce_scatter | solution.py:42
  528.0 76.2 %reduce-scatter.21.cloned.1.call-start = ((), (), s32[]{:S(2)}) async-start(), calls=%async_computation.14 | async-start | bytes 36864 | tf_op jit(solution)/shard_map/reduce_scatter | solution.py:41
Sparse Core Ops, SparseCore 0:
  43.4 20.4 reduce-scatter.10
  67.0 54.6 reduce-scatter.8
  206.6 18.1 reduce-scatter.14
  227.7 54.7 reduce-scatter.12
  367.3 18.1 reduce-scatter.18
  388.4 54.7 reduce-scatter.16
  528.2 18.1 reduce-scatter.22
  549.5 54.7 reduce-scatter.20
where the time goes:
time: 657 us; the launch traced here: 656 us
  blocking collectives  307 us (47%)
  waiting for transfers between devices  297 us (45%)
  matrix products  15.5 us (2%)
  between operations  15 us (2%)
  other arithmetic  14 us (2%)
  local copies, waits for them, and re-layouts  7.5 us (1%)
    reduce_scatter x4, waiting for transfers between devices, apply_tile(): lax.psum_scatter(direct_part, 'col', scatter_dimension=1, tiled=True)  231 us
    psum x4, blocking collectives, gram_factor(): gram = lax.psum(local_gram, ('row', 'col'))  161 us
    all_gather x4, blocking collectives, shards(): row_vectors = lax.all_gather(current, 'col', axis=1, tiled=True)  124 us
    reduce_scatter x4, waiting for transfers between devices, apply_tile(): lax.psum_scatter(transposed_part, 'row', scatter_dimension=1, tiled=True)  65.6 us
    all_gather x4, blocking collectives, shards(): col_vectors = lax.all_gather(current, 'row', axis=1, tiled=True)  21.9 us
  transfers between devices with their start and end apart: 8, of which 8 were waited for; matrix products, arithmetic and copies ran while one was open for 1% of the time, Pallas kernels for 0%

commit v1 on v0

--- a/solution.py
+++ b/solution.py
@@ -61,7 +61,24 @@
     lower = jnp.eye(nvec, dtype=jnp.float32)
     for step in range(ITERS):
         col_vectors = lax.all_gather(current, "row", axis=1, tiled=True)
-        row_vectors = lax.all_gather(current, "col", axis=1, tiled=True)
+        ways, here, k = (lax.axis_size("col"), lax.axis_index("col"), current.shape[1])
+        lengths = [n * ways if d == 1 else n for d, n in enumerate(current.shape)]
+        row_vectors = lax.dynamic_update_slice_in_dim(
+            jnp.zeros(lengths, current.dtype), current, here * k, axis=1
+        )
+        going_up = going_down = current
+        for far in range(1, ways // 2 + 1):
+            going_up = lax.ppermute(going_up, "col", [(d, (d + 1) % ways) for d in range(ways)])
+            row_vectors = lax.dynamic_update_slice_in_dim(
+                row_vectors, going_up, (here - far) % ways * k, axis=1
+            )
+            if 2 * far < ways:
+                going_down = lax.ppermute(
+                    going_down, "col", [(d, (d - 1) % ways) for d in range(ways)]
+                )
+                row_vectors = lax.dynamic_update_slice_in_dim(
+                    row_vectors, going_down, (here + far) % ways * k, axis=1
+                )
         direct_sum, transposed_sum = apply_tile(
             tile, rows_local, cols_local, live, current, col_vectors, row_vectors
         )

time: 657 us -> 631 us (0.960)
  blocking collectives: 307 us -> 182 us
  starting transfers between devices: 0.33 us -> 58.5 us
  waiting for transfers between devices: 297 us -> 335 us
    all_gather x4 -> x0, blocking collectives: 124 us -> none  [shards(): row_vectors = lax.all_gather(current, 'col', axis=1, tiled=True)]
    ppermute x0 -> x28, starting transfers between devices: none -> 58.1 us  [the longest x12 48.1 us: shards(): lax.ppermute(going_down, 'col', [(d, (d - 1) % ways) for d in range(ways)])]
    ppermute x0 -> x28, waiting for transfers between devices: none -> 37.7 us  [the longest x16 37.7 us: shards(): lax.ppermute(going_up, 'col', [(d, (d + 1) % ways) for d in range(ways)])]
  transfers between devices with their start and end apart: 8 -> 36, of which waited for: 8 -> 20; matrix products, arithmetic and copies ran while one was open for 1% -> 2% of each run, Pallas kernels for 0% -> 0%
where the time goes in v1:
time: 631 us; the launch traced here: 630 us
  waiting for transfers between devices  335 us (53%)
  blocking collectives  182 us (29%)
  starting transfers between devices  58.5 us (9%)
  matrix products  16.3 us (3%)
  between operations  15.2 us (2%)
  other arithmetic  14.1 us (2%)
  local copies, waits for them, and re-layouts  8.46 us (1%)
    reduce_scatter x4, waiting for transfers between devices, apply_tile(): lax.psum_scatter(direct_part, 'col', scatter_dimension=1, tiled=True)  231 us
    psum x4, blocking collectives, gram_factor(): gram = lax.psum(local_gram, ('row', 'col'))  160 us
    reduce_scatter x4, waiting for transfers between devices, apply_tile(): lax.psum_scatter(transposed_part, 'row', scatter_dimension=1, tiled=True)  65.6 us
    ppermute x12, starting transfers between devices, shards(): lax.ppermute(going_down, 'col', [(d, (d - 1) % ways) for d in range(ways)])  48.1 us
    ppermute x16, waiting for transfers between devices, shards(): lax.ppermute(going_up, 'col', [(d, (d + 1) % ways) for d in range(ways)])  37.7 us
    all_gather x4, blocking collectives, shards(): col_vectors = lax.all_gather(current, 'row', axis=1, tiled=True)  22 us
  transfers between devices with their start and end apart: 36, of which 20 were waited for; matrix products, arithmetic and copies ran while one was open for 2% of the time, Pallas kernels for 0%

profile of v1, /device:TPU:0, one launch (start us, length us, event | category | flops | bytes accessed | tf_op | source)
XLA Modules:
  0.0 629.7 jit_solution(4906009306303666219)
XLA Ops:
  7.2 3.0 collective-permute-start
  10.3 3.1 collective-permute-start.1
  14.1 5.2 all_gather.12
  21.9 4.7 collective-permute-start.3
  26.6 1.6 collective-permute-done.2
  28.2 4.7 collective-permute-start.5
  32.9 1.6 collective-permute-done.4
  34.5 6.3 collective-permute-done.6
  44.9 16.1 %reduce-scatter.11.cloned.1.call-done = f32[8,128]{1,0:T(8,128)} async-done(((f32[8,512]{1,0:T(8,128)}), f32[8,128]{1,0:T(8,128)}) %reduce-scatter.11.cloned.1.call-update) | async-done | bytes 4112 | tf_op jit(solution)/shard_map/reduce_scatter | solution.py:42
  61.0 57.9 %reduce-scatter.9.cloned.1.call-done = f32[8,128]{1,0:T(8,128)} async-done(((f32[8,1024]{1,0:T(8,128)}), f32[8,128]{1,0:T(8,128)}) %reduce-scatter.9.cloned.1.call-update) | async-done | bytes 4112 | tf_op jit(solution)/shard_map/reduce_scatter | solution.py:41
  119.7 40.1 %psum.28 = f32[8,8]{0,1:T(8,128)S(1)} all-reduce(f32[8,8]{0,1:T(8,128)S(1)} %fusion.162), channel_id=1, replica_groups=mesh['row'=4,'col'=8] {'row','col'}, use_global_device_ids=true, to_apply=%region_2.3 | all-reduce | flops 64 | bytes 512 | tf_op jit(solution)/shard_map/psum | solution.py:50
  162.8 2.3 collective-permute-start.7
  165.1 2.5 collective-permute-start.8
  167.5 5.5 all_gather.13
  175.2 4.7 collective-permute-start.10
  179.9 1.6 collective-permute-done.9
  181.5 4.7 collective-permute-start.12
  186.2 1.6 collective-permute-done.11
  187.8 6.3 collective-permute-done.13
  194.1 1.0 convolution_bitcast_fusion.2
  197.5 16.5 %reduce-scatter.15.cloned.1.call-done = f32[8,128]{1,0:T(8,128)} async-done(((f32[8,512]{1,0:T(8,128)}), f32[8,128]{1,0:T(8,128)}) %reduce-scatter.15.cloned.1.call-update) | async-done | bytes 4112 | tf_op jit(solution)/shard_map/reduce_scatter | solution.py:42
  214.0 57.8 %reduce-scatter.13.cloned.1.call-done = f32[8,128]{1,0:T(8,128)} async-done(((f32[8,1024]{1,0:T(8,128)}), f32[8,128]{1,0:T(8,128)}) %reduce-scatter.13.cloned.1.call-update) | async-done | bytes 4112 | tf_op jit(solution)/shard_map/reduce_scatter | solution.py:41
  272.6 40.1 %psum.29 = f32[8,8]{0,1:T(8,128)S(1)} all-reduce(f32[8,8]{0,1:T(8,128)S(1)} %fusion.163), channel_id=1, replica_groups=mesh['row'=4,'col'=8] {'row','col'}, use_global_device_ids=true, to_apply=%region_7.10 | all-reduce | flops 64 | bytes 512 | tf_op jit(solution)/shard_map/psum | solution.py:50
  315.6 2.3 collective-permute-start.14
  317.9 2.5 collective-permute-start.15
  320.3 5.7 all_gather.14
  328.2 4.7 collective-permute-start.17
  332.9 1.6 collective-permute-done.16
  334.5 4.7 collective-permute-start.19
  339.2 1.6 collective-permute-done.18
  340.8 6.3 collective-permute-done.20
  347.1 1.0 convolution_bitcast_fusion.1
  350.5 16.5 %reduce-scatter.19.cloned.1.call-done = f32[8,128]{1,0:T(8,128)} async-done(((f32[8,512]{1,0:T(8,128)}), f32[8,128]{1,0:T(8,128)}) %reduce-scatter.19.cloned.1.call-update) | async-done | bytes 4112 | tf_op jit(solution)/shard_map/reduce_scatter | solution.py:42
  367.0 57.8 %reduce-scatter.17.cloned.1.call-done = f32[8,128]{1,0:T(8,128)} async-done(((f32[8,1024]{1,0:T(8,128)}), f32[8,128]{1,0:T(8,128)}) %reduce-scatter.17.cloned.1.call-update) | async-done | bytes 4112 | tf_op jit(solution)/shard_map/reduce_scatter | solution.py:41
  425.6 40.1 %psum.30 = f32[8,8]{0,1:T(8,128)S(1)} all-reduce(f32[8,8]{0,1:T(8,128)S(1)} %fusion.164), channel_id=1, replica_groups=mesh['row'=4,'col'=8] {'row','col'}, use_global_device_ids=true, to_apply=%region_10.13 | all-reduce | flops 64 | bytes 512 | tf_op jit(solution)/shard_map/psum | solution.py:50
  468.6 2.3 collective-permute-start.21
  470.9 2.5 collective-permute-start.22
  473.4 5.5 all_gather.15
  481.1 4.7 collective-permute-start.24
  485.8 1.6 collective-permute-done.23
  487.3 4.7 collective-permute-start.26
  492.1 1.6 collective-permute-done.25
  493.7 6.3 collective-permute-done.27
  499.9 1.0 convolution_bitcast_fusion
  503.3 16.5 %reduce-scatter.23.cloned.1.call-done = f32[8,128]{1,0:T(8,128)} async-done(((f32[8,512]{1,0:T(8,128)}), f32[8,128]{1,0:T(8,128)}) %reduce-scatter.23.cloned.1.call-update) | async-done | bytes 4112 | tf_op jit(solution)/shard_map/reduce_scatter | solution.py:42
  519.8 58.0 %reduce-scatter.21.cloned.1.call-done = f32[8,128]{1,0:T(8,128)} async-done(((f32[8,1024]{1,0:T(8,128)}), f32[8,128]{1,0:T(8,128)}) %reduce-scatter.21.cloned.1.call-update) | async-done | bytes 4112 | tf_op jit(solution)/shard_map/reduce_scatter | solution.py:41
  578.6 40.1 %psum.31 = f32[8,8]{0,1:T(8,128)S(1)} all-reduce(f32[8,8]{0,1:T(8,128)S(1)} %fusion.165), channel_id=1, replica_groups=mesh['row'=4,'col'=8] {'row','col'}, use_global_device_ids=true, to_apply=%region_13.16 | all-reduce | flops 64 | bytes 512 | tf_op jit(solution)/shard_map/psum | solution.py:50
  620.2 1.2 select_bitcast_fusion
  (163 shorter events, 35.2 us)
Async XLA Ops:
  7.2 13.7 %copy-start = (f32[1,1,8,128,128]{4,3,2,1,0:T(8,128)S(1)}, f32[1,1,8,128,128]{4,3,2,1,0:T(8,128)}, u32[]{:S(2)}) copy-start(f32[1,1,8,128,128]{4,3,2,1,0:T(8,128)} %param.11) | copy-start | bytes 1572868
  7.2 53.8 %reduce-scatter.11.cloned.1.call-start = ((), (), s32[]{:S(2)}) async-start(), calls=%async_computation.9 | async-start | bytes 20480 | tf_op jit(solution)/shard_map/reduce_scatter | solution.py:42
  7.2 14.6 %collective-permute-start = (f32[8,128]{1,0:T(8,128)}, f32[8,128]{1,0:T(8,128)S(1)}, u32[]{:S(2)}, u32[]{:S(2)}) collective-permute-start(f32[8,128]{1,0:T(8,128)} %param.9), channel_id=1, source_target_pairs={{0,1},{1,2},{2,3},{3,4},{4,5},{5,6},{6,7},{7,0},{8,9},{9,10},{10,1... | collective-permute-start | bytes 12296 | tf_op jit(solution)/shard_map/ppermute | solution.py:71
  10.3 11.6 %collective-permute-start.1 = (f32[8,128]{1,0:T(8,128)}, f32[8,128]{1,0:T(8,128)S(1)}, u32[]{:S(2)}, u32[]{:S(2)}) collective-permute-start(f32[8,128]{1,0:T(8,128)} %param.9), channel_id=1, source_target_pairs={{0,7},{1,0},{2,1},{3,2},{4,3},{5,4},{6,5},{7,6},{8,15},{9,8},{10,9... | collective-permute-start | bytes 12296 | tf_op jit(solution)/shard_map/ppermute | solution.py:76
  13.4 0.7 copy-start.1
  20.0 0.7 copy-start.2
  21.8 6.4 %collective-permute-start.2 = (f32[8,128]{1,0:T(8,128)S(1)}, f32[8,128]{1,0:T(8,128)S(1)}, u32[]{:S(2)}, u32[]{:S(2)}) collective-permute-start(f32[8,128]{1,0:T(8,128)S(1)} %collective-permute-done), channel_id=1, source_target_pairs={{0,1},{1,2},{2,3},{3,4},{4,5},{5,6},{6,7},{7,0},{8,9},{9,10},{10,1... | collective-permute-start | bytes 12296 | tf_op jit(solution)/shard_map/ppermute | solution.py:71
  21.9 6.3 collective-permute-start.3
  28.2 6.3 %collective-permute-start.4 = (f32[8,128]{1,0:T(8,128)S(1)}, f32[8,128]{1,0:T(8,128)S(1)}, u32[]{:S(2)}, u32[]{:S(2)}) collective-permute-start(f32[8,128]{1,0:T(8,128)S(1)} %collective-permute-done.2), channel_id=1, source_target_pairs={{0,1},{1,2},{2,3},{3,4},{4,5},{5,6},{6,7},{7,0},{8,9},{9,10},{10,1... | collective-permute-start | bytes 12296 | tf_op jit(solution)/shard_map/ppermute | solution.py:71
  28.2 6.3 %collective-permute-start.5 = (f32[8,128]{1,0:T(8,128)S(1)}, f32[8,128]{1,0:T(8,128)S(1)}, u32[]{:S(2)}, u32[]{:S(2)}) collective-permute-start(f32[8,128]{1,0:T(8,128)S(1)} %collective-permute-done.3), channel_id=1, source_target_pairs={{0,7},{1,0},{2,1},{3,2},{4,3},{5,4},{6,5},{7,6},{8,15},{9,8},{10,9... | collective-permute-start | bytes 12296 | tf_op jit(solution)/shard_map/ppermute | solution.py:76
  34.5 6.3 %collective-permute-start.6 = (f32[8,128]{1,0:T(8,128)S(1)}, f32[8,128]{1,0:T(8,128)S(1)}, u32[]{:S(2)}, u32[]{:S(2)}) collective-permute-start(f32[8,128]{1,0:T(8,128)S(1)} %collective-permute-done.4), channel_id=1, source_target_pairs={{0,1},{1,2},{2,3},{3,4},{4,5},{5,6},{6,7},{7,0},{8,9},{9,10},{10,1... | collective-permute-start | bytes 12296 | tf_op jit(solution)/shard_map/ppermute | solution.py:71
  40.8 0.7 copy-start.3
  44.0 74.9 %reduce-scatter.9.cloned.1.call-start = ((), (), s32[]{:S(2)}) async-start(), calls=%async_computation.8 | async-start | bytes 36864 | tf_op jit(solution)/shard_map/reduce_scatter | solution.py:41
  44.8 74.1 %copy-start.4 = (f32[128]{0:T(128)S(1)}, f32[128]{0:T(128)}, u32[]{:S(2)}) copy-start(f32[128]{0:T(128)} %param.10) | copy-start | bytes 1540
  44.8 169.1 %reduce-scatter.15.cloned.1.call-start = ((), (), s32[]{:S(2)}) async-start(), calls=%async_computation.11 | async-start | bytes 20480 | tf_op jit(solution)/shard_map/reduce_scatter | solution.py:42
  162.8 12.4 %collective-permute-start.7 = (f32[8,128]{1,0:T(8,128)S(1)}, f32[8,128]{1,0:T(8,128)S(1)}, u32[]{:S(2)}, u32[]{:S(2)}) collective-permute-start(f32[8,128]{1,0:T(8,128)S(1)} %get-tuple-element.7), channel_id=1, source_target_pairs={{0,1},{1,2},{2,3},{3,4},{4,5},{5,6},{6,7},{7,0},{8,9},{9,10},{10,1... | collective-permute-start | bytes 12296 | tf_op jit(solution)/shard_map/ppermute | solution.py:71
  165.1 10.1 %collective-permute-start.8 = (f32[8,128]{1,0:T(8,128)S(1)}, f32[8,128]{1,0:T(8,128)S(1)}, u32[]{:S(2)}, u32[]{:S(2)}) collective-permute-start(f32[8,128]{1,0:T(8,128)S(1)} %get-tuple-element.7), channel_id=1, source_target_pairs={{0,7},{1,0},{2,1},{3,2},{4,3},{5,4},{6,5},{7,6},{8,15},{9,8},{10,9... | collective-permute-start | bytes 12296 | tf_op jit(solution)/shard_map/ppermute | solution.py:76
  175.1 6.3 %collective-permute-start.9 = (f32[8,128]{1,0:T(8,128)S(1)}, f32[8,128]{1,0:T(8,128)S(1)}, u32[]{:S(2)}, u32[]{:S(2)}) collective-permute-start(f32[8,128]{1,0:T(8,128)S(1)} %collective-permute-done.7), channel_id=1, source_target_pairs={{0,1},{1,2},{2,3},{3,4},{4,5},{5,6},{6,7},{7,0},{8,9},{9,10},{10,1... | collective-permute-start | bytes 12296 | tf_op jit(solution)/shard_map/ppermute | solution.py:71
  175.2 6.3 collective-permute-start.10
  181.5 6.3 %collective-permute-start.11 = (f32[8,128]{1,0:T(8,128)S(1)}, f32[8,128]{1,0:T(8,128)S(1)}, u32[]{:S(2)}, u32[]{:S(2)}) collective-permute-start(f32[8,128]{1,0:T(8,128)S(1)} %collective-permute-done.9), channel_id=1, source_target_pairs={{0,1},{1,2},{2,3},{3,4},{4,5},{5,6},{6,7},{7,0},{8,9},{9,10},{10,1... | collective-permute-start | bytes 12296 | tf_op jit(solution)/shard_map/ppermute | solution.py:71
  181.5 6.3 %collective-permute-start.12 = (f32[8,128]{1,0:T(8,128)S(1)}, f32[8,128]{1,0:T(8,128)S(1)}, u32[]{:S(2)}, u32[]{:S(2)}) collective-permute-start(f32[8,128]{1,0:T(8,128)S(1)} %collective-permute-done.10), channel_id=1, source_target_pairs={{0,7},{1,0},{2,1},{3,2},{4,3},{5,4},{6,5},{7,6},{8,15},{9,8},{10,9... | collective-permute-start | bytes 12296 | tf_op jit(solution)/shard_map/ppermute | solution.py:76
  187.8 6.3 %collective-permute-start.13 = (f32[8,128]{1,0:T(8,128)S(1)}, f32[8,128]{1,0:T(8,128)S(1)}, u32[]{:S(2)}, u32[]{:S(2)}) collective-permute-start(f32[8,128]{1,0:T(8,128)S(1)} %collective-permute-done.11), channel_id=1, source_target_pairs={{0,1},{1,2},{2,3},{3,4},{4,5},{5,6},{6,7},{7,0},{8,9},{9,10},{10,1... | collective-permute-start | bytes 12296 | tf_op jit(solution)/shard_map/ppermute | solution.py:71
  196.6 75.1 %reduce-scatter.13.cloned.1.call-start = ((), (), s32[]{:S(2)}) async-start(), calls=%async_computation.10 | async-start | bytes 36864 | tf_op jit(solution)/shard_map/reduce_scatter | solution.py:41
  197.5 169.5 %reduce-scatter.19.cloned.1.call-start = ((), (), s32[]{:S(2)}) async-start(), calls=%async_computation.13 | async-start | bytes 20480 | tf_op jit(solution)/shard_map/reduce_scatter | solution.py:42
  315.6 12.6 %collective-permute-start.14 = (f32[8,128]{1,0:T(8,128)S(1)}, f32[8,128]{1,0:T(8,128)S(1)}, u32[]{:S(2)}, u32[]{:S(2)}) collective-permute-start(f32[8,128]{1,0:T(8,128)S(1)} %get-tuple-element.9), channel_id=1, source_target_pairs={{0,1},{1,2},{2,3},{3,4},{4,5},{5,6},{6,7},{7,0},{8,9},{9,10},{10,1... | collective-permute-start | bytes 12296 | tf_op jit(solution)/shard_map/ppermute | solution.py:71
  317.9 10.3 %collective-permute-start.15 = (f32[8,128]{1,0:T(8,128)S(1)}, f32[8,128]{1,0:T(8,128)S(1)}, u32[]{:S(2)}, u32[]{:S(2)}) collective-permute-start(f32[8,128]{1,0:T(8,128)S(1)} %get-tuple-element.9), channel_id=1, source_target_pairs={{0,7},{1,0},{2,1},{3,2},{4,3},{5,4},{6,5},{7,6},{8,15},{9,8},{10,9... | collective-permute-start | bytes 12296 | tf_op jit(solution)/shard_map/ppermute | solution.py:76
  328.1 6.3 %collective-permute-start.16 = (f32[8,128]{1,0:T(8,128)S(1)}, f32[8,128]{1,0:T(8,128)S(1)}, u32[]{:S(2)}, u32[]{:S(2)}) collective-permute-start(f32[8,128]{1,0:T(8,128)S(1)} %collective-permute-done.14), channel_id=1, source_target_pairs={{0,1},{1,2},{2,3},{3,4},{4,5},{5,6},{6,7},{7,0},{8,9},{9,10},{10,1... | collective-permute-start | bytes 12296 | tf_op jit(solution)/shard_map/ppermute | solution.py:71
  328.2 6.3 collective-permute-start.17
  334.5 6.3 %collective-permute-start.18 = (f32[8,128]{1,0:T(8,128)S(1)}, f32[8,128]{1,0:T(8,128)S(1)}, u32[]{:S(2)}, u32[]{:S(2)}) collective-permute-start(f32[8,128]{1,0:T(8,128)S(1)} %collective-permute-done.16), channel_id=1, source_target_pairs={{0,1},{1,2},{2,3},{3,4},{4,5},{5,6},{6,7},{7,0},{8,9},{9,10},{10,1... | collective-permute-start | bytes 12296 | tf_op jit(solution)/shard_map/ppermute | solution.py:71
  334.5 6.3 %collective-permute-start.19 = (f32[8,128]{1,0:T(8,128)S(1)}, f32[8,128]{1,0:T(8,128)S(1)}, u32[]{:S(2)}, u32[]{:S(2)}) collective-permute-start(f32[8,128]{1,0:T(8,128)S(1)} %collective-permute-done.17), channel_id=1, source_target_pairs={{0,7},{1,0},{2,1},{3,2},{4,3},{5,4},{6,5},{7,6},{8,15},{9,8},{10,9... | collective-permute-start | bytes 12296 | tf_op jit(solution)/shard_map/ppermute | solution.py:76
  340.8 6.3 %collective-permute-start.20 = (f32[8,128]{1,0:T(8,128)S(1)}, f32[8,128]{1,0:T(8,128)S(1)}, u32[]{:S(2)}, u32[]{:S(2)}) collective-permute-start(f32[8,128]{1,0:T(8,128)S(1)} %collective-permute-done.18), channel_id=1, source_target_pairs={{0,1},{1,2},{2,3},{3,4},{4,5},{5,6},{6,7},{7,0},{8,9},{9,10},{10,1... | collective-permute-start | bytes 12296 | tf_op jit(solution)/shard_map/ppermute | solution.py:71
  349.6 75.2 %reduce-scatter.17.cloned.1.call-start = ((), (), s32[]{:S(2)}) async-start(), calls=%async_computation.12 | async-start | bytes 36864 | tf_op jit(solution)/shard_map/reduce_scatter | solution.py:41
  350.4 169.4 %reduce-scatter.23.cloned.1.call-start = ((), (), s32[]{:S(2)}) async-start(), calls=%async_computation.15 | async-start | bytes 20480 | tf_op jit(solution)/shard_map/reduce_scatter | solution.py:42
  468.6 12.4 %collective-permute-start.21 = (f32[8,128]{1,0:T(8,128)S(1)}, f32[8,128]{1,0:T(8,128)S(1)}, u32[]{:S(2)}, u32[]{:S(2)}) collective-permute-start(f32[8,128]{1,0:T(8,128)S(1)} %get-tuple-element.11), channel_id=1, source_target_pairs={{0,1},{1,2},{2,3},{3,4},{4,5},{5,6},{6,7},{7,0},{8,9},{9,10},{10,1... | collective-permute-start | bytes 12296 | tf_op jit(solution)/shard_map/ppermute | solution.py:71
  470.9 10.1 %collective-permute-start.22 = (f32[8,128]{1,0:T(8,128)S(1)}, f32[8,128]{1,0:T(8,128)S(1)}, u32[]{:S(2)}, u32[]{:S(2)}) collective-permute-start(f32[8,128]{1,0:T(8,128)S(1)} %get-tuple-element.11), channel_id=1, source_target_pairs={{0,7},{1,0},{2,1},{3,2},{4,3},{5,4},{6,5},{7,6},{8,15},{9,8},{10,9... | collective-permute-start | bytes 12296 | tf_op jit(solution)/shard_map/ppermute | solution.py:76
  481.0 6.3 %collective-permute-start.23 = (f32[8,128]{1,0:T(8,128)S(1)}, f32[8,128]{1,0:T(8,128)S(1)}, u32[]{:S(2)}, u32[]{:S(2)}) collective-permute-start(f32[8,128]{1,0:T(8,128)S(1)} %collective-permute-done.21), channel_id=1, source_target_pairs={{0,1},{1,2},{2,3},{3,4},{4,5},{5,6},{6,7},{7,0},{8,9},{9,10},{10,1... | collective-permute-start | bytes 12296 | tf_op jit(solution)/shard_map/ppermute | solution.py:71
  481.1 6.3 collective-permute-start.24
  487.3 6.3 %collective-permute-start.25 = (f32[8,128]{1,0:T(8,128)S(1)}, f32[8,128]{1,0:T(8,128)S(1)}, u32[]{:S(2)}, u32[]{:S(2)}) collective-permute-start(f32[8,128]{1,0:T(8,128)S(1)} %collective-permute-done.23), channel_id=1, source_target_pairs={{0,1},{1,2},{2,3},{3,4},{4,5},{5,6},{6,7},{7,0},{8,9},{9,10},{10,1... | collective-permute-start | bytes 12296 | tf_op jit(solution)/shard_map/ppermute | solution.py:71
  487.3 6.3 %collective-permute-start.26 = (f32[8,128]{1,0:T(8,128)S(1)}, f32[8,128]{1,0:T(8,128)S(1)}, u32[]{:S(2)}, u32[]{:S(2)}) collective-permute-start(f32[8,128]{1,0:T(8,128)S(1)} %collective-permute-done.24), channel_id=1, source_target_pairs={{0,7},{1,0},{2,1},{3,2},{4,3},{5,4},{6,5},{7,6},{8,15},{9,8},{10,9... | collective-permute-start | bytes 12296 | tf_op jit(solution)/shard_map/ppermute | solution.py:76
  493.6 6.3 %collective-permute-start.27 = (f32[8,128]{1,0:T(8,128)S(1)}, f32[8,128]{1,0:T(8,128)S(1)}, u32[]{:S(2)}, u32[]{:S(2)}) collective-permute-start(f32[8,128]{1,0:T(8,128)S(1)} %collective-permute-done.25), channel_id=1, source_target_pairs={{0,1},{1,2},{2,3},{3,4},{4,5},{5,6},{6,7},{7,0},{8,9},{9,10},{10,1... | collective-permute-start | bytes 12296 | tf_op jit(solution)/shard_map/ppermute | solution.py:71
  502.5 75.3 %reduce-scatter.21.cloned.1.call-start = ((), (), s32[]{:S(2)}) async-start(), calls=%async_computation.14 | async-start | bytes 36864 | tf_op jit(solution)/shard_map/reduce_scatter | solution.py:41
Sparse Core Ops, SparseCore 0:
  44.1 16.8 reduce-scatter.10
  64.1 54.7 reduce-scatter.8
  196.7 17.2 reduce-scatter.14
  217.0 54.7 reduce-scatter.12
  349.7 17.2 reduce-scatter.18
  369.9 54.7 reduce-scatter.16
  502.6 17.2 reduce-scatter.22
  523.0 54.7 reduce-scatter.20
